TPU v7x, 32 devices: a whole 2x2x4 slice. The times are simulated.
32 devices in a mesh: row: 8 (over z, y), col: 2 (over core), layer: 2 (over x).
Axes of the slice: x: 2, y: 2, z: 4, core: 2. Of those that a mesh axis runs over, the one named last changes fastest.
Arguments:
- matrix: float32 [1, 8, 256, 4, 2, 256], P(None, 'row', None, None, 'col'), may hold values from -8 to 113.137085, as said below
Outputs:
- factored: float32 [1, 8, 256, 4, 2, 256], P(None, 'row', None, 'layer', 'col')
Inputs may be any that keep to these rules, and one draw needn't show every extreme that they name: `matrix`: viewed as in the first step it is symmetric, its leading 2 * 256 x 2 * 256 block is positive definite, and its diagonal entries lie between 2.5 and 5 times the square root of 512.
All inputs are finite; a program needn't handle non-finite values.
Results may differ from a plain program's by a relative error of at most 0.000059.
Values sent between devices are 32-bit elements; how exact they have to be, the bound alone decides.
No kernel may reach another device: no remote copies, remote signals or barrier semaphores. Data moves between devices by JAX's collectives and lax.ppermute only.
A program may use at most 128 MiB of HBM per device.

v0:
```python
import jax
import jax.numpy as jnp
from jax import lax
from jax.sharding import PartitionSpec as P

HIGH = lax.Precision.HIGHEST


def from_root(shard, axis, root):
    mine = lax.axis_index(axis) == root
    return lax.psum(jnp.where(mine, shard, jnp.zeros_like(shard)), axis)


def factor_block(diag_block):
    lower_fac = jnp.linalg.cholesky(diag_block)
    identity = jnp.eye(diag_block.shape[0], dtype=jnp.float32)
    inverse = lax.linalg.triangular_solve(lower_fac, identity, left_side=True, lower=True)
    return (lower_fac, inverse)


def on_device(matrix):
    row_total = lax.axis_size("row")
    col_total = lax.axis_size("col")
    layer_total = lax.axis_size("layer")
    grid_row = lax.axis_index("row")
    grid_col = lax.axis_index("col")
    grid_layer = lax.axis_index("layer")
    row_blocks = matrix.shape[0]
    block_size = matrix.shape[2]
    col_blocks = matrix.shape[3]
    half = block_size // layer_total
    owned = col_blocks // layer_total
    rows = row_blocks * block_size
    tile = matrix.reshape(rows, col_blocks * block_size)
    row_ids = jnp.arange(rows) // block_size * row_total + grid_row
    column = tile[:, :block_size]
    pending = None
    total = None
    panels = []
    for section in range(2):
        diag_block = from_root(column, "row", section % row_total)
        lower_fac, inverse = factor_block(diag_block)
        solved = jnp.dot(column, inverse.T, precision=HIGH, preferred_element_type=jnp.float32)
        repeated = jnp.tile(lower_fac, (row_blocks, 1))
        complete = jnp.where(
            row_ids[:, None] > section,
            solved,
            jnp.where(row_ids[:, None] == section, repeated, 0.0),
        )
        panels.append(complete)
        share = lax.dynamic_slice_in_dim(complete, grid_layer * half, half, 1)
        share = from_root(share, "col", section % col_total)
        gathered = lax.all_gather(
            share.reshape(row_blocks, 1, block_size, half), "row", axis=1, tiled=True
        )
        grouped = gathered.reshape(col_blocks, col_total, block_size, half)
        picked = lax.dynamic_index_in_dim(grouped, grid_col, 1, keepdims=False).reshape(
            col_blocks * block_size, half
        )
        update = lax.dot_general(
            share,
            picked,
            (((1,), (1,)), ((), ())),
            precision=HIGH,
            preferred_element_type=jnp.float32,
        )
        if section == 0:
            head = lax.psum(update[:, :block_size], "layer")
            column = tile[:, :block_size] - head
            pending = update
        else:
            total = pending + update
    reduced = lax.psum_scatter(
        total.reshape(rows, col_blocks, block_size), "layer", scatter_dimension=1, tiled=True
    )
    own_part = (
        lax.dynamic_slice_in_dim(
            tile.reshape(rows, col_blocks, block_size), grid_layer * owned, owned, 1
        )
        - reduced
    )
    replacement = jnp.where(grid_col == 0, panels[0], panels[1])
    global_ids = (grid_layer * owned + jnp.arange(owned)) * col_total + grid_col
    result = jnp.where((global_ids < 2)[None, :, None], replacement[:, None, :], own_part)
    return result.reshape(row_blocks, 1, block_size, owned, 1, block_size)


def solution(mesh):
    in_specs = (P(None, "row", None, None, "col", None),)
    out_specs = P(None, "row", None, "layer", "col", None)
    return jax.shard_map(
        on_device, mesh=mesh, in_specs=in_specs, out_specs=out_specs, check_vma=False
    )
```

profile of v0, /device:TPU:0, one launch (start us, length us, event | category | flops | bytes accessed | tf_op | source)
XLA Modules:
  0.0 472.5 jit_solution(6674159370767984335)
XLA Ops:
  6.5 2.3 copy.16
  9.8 74.7 %all-reduce.7.cloned.1.call-done = f32[256,256]{0,1:T(8,128)} async-done(((f32[256,256]{0,1:T(8,128)}), f32[256,256]{0,1:T(8,128)}) %all-reduce.7.cloned.1.call-update) | async-done | bytes 262160 | tf_op jit(solution)/shard_map/psum | solution.py:11
  84.4 1.1 copy.17
  85.7 11.7 %cholesky.130 = f32[128,128]{1,0:T(8,128)S(1)} custom-call(f32[128,128]{1,0:T(8,128)S(1)} %cholesky.194), custom_call_target="Cholesky" | custom-call | tf_op jit(solution)/shard_map/jit(cholesky)/cholesky | solution.py:15
  97.4 9.8 %custom-call.13 = f32[1,128,128]{1,2,0:T(8,128)S(1)} custom-call(f32[1,128,128]{2,1,0:T(8,128)S(1)} %get-tuple-element.62), custom_call_target="InvertDiagBlocksLowerTriangular" | custom-call | tf_op jit(solution)/shard_map/jit(cholesky)/cholesky | solution.py:15
  107.7 11.7 %cholesky.147 = f32[128,128]{1,0:T(8,128)S(1)} custom-call(f32[128,128]{1,0:T(8,128)S(1)} %convolution_subtract_fusion.3), custom_call_target="Cholesky" | custom-call | tf_op jit(solution)/shard_map/jit(cholesky)/cholesky | solution.py:15
  122.0 4.8 %while.4 = (s32[]{:T(128)}, f32[256,256]{0,1:T(8,128)S(1)}, s32[2,2]{1,0:T(2,128)S(1)}, f32[2,128,128]{2,1,0:T(8,128)S(1)}, s32[]{:T(128)}) while((s32[]{:T(128)}, f32[256,256]{0,1:T(8,128)S(1)}, s32[2,2]{1,0:T(2,128)S(1)}, f32[2,128,128]{2,1,0:T(8,128)S(1)}, s32[]{:T(128)}) %tuple.46), condition=%wide.while_cond, body=%wide.while_body.sunk | while | flops 2 | bytes 393321 | solution.py:17
  123.1 1.4 dynamic-slice.13
  125.3 1.4 dynamic-slice.13
  126.8 19.7 %custom-call.14 = f32[2,128,128]{1,2,0:T(8,128)S(1)} custom-call(f32[2,128,128]{2,1,0:T(8,128)S(1)} %get-tuple-element.21), custom_call_target="InvertDiagBlocksLowerTriangular" | custom-call | tf_op jit(solution)/shard_map/triangular_solve/custom-call.0 | solution.py:17
  148.6 17.2 %all-reduce.9.cloned.1.call-done = f32[256,128]{0,1:T(8,128)} async-done(((f32[256,128]{0,1:T(8,128)}), f32[256,128]{0,1:T(8,128)}) %all-reduce.9.cloned.1.call-update) | async-done | bytes 131088 | tf_op jit(solution)/shard_map/psum | solution.py:11
  165.9 42.6 %all-gather.5.cloned.1.call-done = f32[2048,128]{0,1:T(8,128)} async-done(((f32[256,128]{0,1:T(8,128)}), f32[2048,128]{0,1:T(8,128)}) %all-gather.5.cloned.1.call-update) | async-done | bytes 1048592 | tf_op jit(solution)/shard_map/all_gather | solution.py:53
  208.5 2.1 reshape.86
  210.6 1.6 dynamic-slice_reduce_fusion.1
  215.1 22.4 %all-reduce.11.cloned.1.call-done = f32[256,256]{0,1:T(8,128)} async-done(((f32[256,256]{0,1:T(8,128)}), f32[256,256]{0,1:T(8,128)}) %all-reduce.11.cloned.1.call-update) | async-done | bytes 262160 | tf_op jit(solution)/shard_map/psum | solution.py:68
  237.5 1.7 broadcast_select_fusion
  239.5 72.3 %all-reduce.13.cloned.1.call-done = f32[256,256]{0,1:T(8,128)} async-done(((f32[256,256]{0,1:T(8,128)}), f32[256,256]{0,1:T(8,128)}) %all-reduce.13.cloned.1.call-update) | async-done | bytes 262160 | tf_op jit(solution)/shard_map/psum | solution.py:11
  313.0 11.7 %cholesky.164 = f32[128,128]{1,0:T(8,128)S(1)} custom-call(f32[128,128]{1,0:T(8,128)S(1)} %cholesky.197), custom_call_target="Cholesky" | custom-call | tf_op jit(solution)/shard_map/jit(cholesky)/cholesky | solution.py:15
  324.8 9.8 %custom-call.15 = f32[1,128,128]{1,2,0:T(8,128)S(1)} custom-call(f32[1,128,128]{2,1,0:T(8,128)S(1)} %get-tuple-element.60), custom_call_target="InvertDiagBlocksLowerTriangular" | custom-call | tf_op jit(solution)/shard_map/jit(cholesky)/cholesky | solution.py:15
  335.1 11.7 %cholesky.181 = f32[128,128]{1,0:T(8,128)S(1)} custom-call(f32[128,128]{1,0:T(8,128)S(1)} %convolution_subtract_fusion.2), custom_call_target="Cholesky" | custom-call | tf_op jit(solution)/shard_map/jit(cholesky)/cholesky | solution.py:15
  349.8 4.4 while.5
  350.7 1.4 dynamic-slice.15
  352.8 1.4 dynamic-slice.15
  354.2 19.7 %custom-call.16 = f32[2,128,128]{1,2,0:T(8,128)S(1)} custom-call(f32[2,128,128]{2,1,0:T(8,128)S(1)} %get-tuple-element.22), custom_call_target="InvertDiagBlocksLowerTriangular" | custom-call | tf_op jit(solution)/shard_map/triangular_solve/custom-call.0 | solution.py:17
  376.7 17.2 %all-reduce.15.cloned.1.call-done = f32[256,128]{0,1:T(8,128)} async-done(((f32[256,128]{0,1:T(8,128)}), f32[256,128]{0,1:T(8,128)}) %all-reduce.15.cloned.1.call-update) | async-done | bytes 131088 | tf_op jit(solution)/shard_map/psum | solution.py:11
  393.9 42.6 %all-gather.7.cloned.1.call-done = f32[2048,128]{0,1:T(8,128)} async-done(((f32[256,128]{0,1:T(8,128)}), f32[2048,128]{0,1:T(8,128)}) %all-gather.7.cloned.1.call-update) | async-done | bytes 1048592 | tf_op jit(solution)/shard_map/all_gather | solution.py:53
  436.6 2.1 reshape.89
  438.7 1.6 dynamic-slice_reduce_fusion
  443.4 1.2 copy-done
  445.0 17.9 %reduce-scatter.2.cloned.1.call-done = f32[256,2,256]{2,0,1:T(8,128)} async-done(((f32[256,4,256]{2,0,1:T(8,128)}), f32[256,2,256]{2,0,1:T(8,128)}) %reduce-scatter.2.cloned.1.call-update) | async-done | bytes 524304 | tf_op jit(solution)/shard_map/reduce_scatter | solution.py:73
  462.9 1.2 fusion.2
  464.1 1.3 copy.32
  (101 shorter events, 20.2 us)
Async XLA Ops:
  6.5 77.9 %all-reduce.7.cloned.1.call-start = ((), (), s32[]{:S(2)}) async-start(), calls=%async_computation.1 | async-start | bytes 524288 | tf_op jit(solution)/shard_map/psum | solution.py:11
  9.6 156.2 %all-reduce.9.cloned.1.call-start = ((), (), s32[]{:S(2)}) async-start(), calls=%async_computation.2 | async-start | bytes 262144 | tf_op jit(solution)/shard_map/psum | solution.py:11
  84.4 1.2 copy-start.1
  148.5 60.0 %all-gather.5.cloned.1.call-start = ((), (), s32[]{:S(2)}) async-start(), calls=%async_computation.7 | async-start | bytes 1179648 | tf_op jit(solution)/shard_map/all_gather | solution.py:53
  165.8 71.7 %all-reduce.11.cloned.1.call-start = ((), (), s32[]{:S(2)}) async-start(), calls=%async_computation.3 | async-start | bytes 524288 | tf_op jit(solution)/shard_map/psum | solution.py:68
  212.2 0.9 copy-start.4
  215.0 96.7 %all-reduce.13.cloned.1.call-start = ((), (), s32[]{:S(2)}) async-start(), calls=%async_computation.4 | async-start | bytes 524288 | tf_op jit(solution)/shard_map/psum | solution.py:11
  239.2 154.7 %all-reduce.15.cloned.1.call-start = ((), (), s32[]{:S(2)}) async-start(), calls=%async_computation.5 | async-start | bytes 262144 | tf_op jit(solution)/shard_map/psum | solution.py:11
  311.8 1.2 copy-start.2
  374.6 1.0 copy-start.3
  376.6 59.9 %all-gather.7.cloned.1.call-start = ((), (), s32[]{:S(2)}) async-start(), calls=%async_computation.8 | async-start | bytes 1179648 | tf_op jit(solution)/shard_map/all_gather | solution.py:53
  393.9 69.0 %reduce-scatter.2.cloned.1.call-start = ((), (), s32[]{:S(2)}) async-start(), calls=%async_computation.6 | async-start | bytes 1572864 | tf_op jit(solution)/shard_map/reduce_scatter | solution.py:73
  440.3 0.9 copy-start.5
  443.3 1.2 copy-start
Sparse Core Ops, SparseCore 0:
  10.7 73.7 all-reduce.6
  148.7 17.0 all-reduce.8
  167.8 40.5 all-gather.4
  215.2 22.2 all-reduce.10
  240.7 71.0 all-reduce.12
  376.7 17.0 all-reduce.14
  395.9 40.5 all-gather.6
  443.5 19.3 reduce-scatter.1
where the time goes:
time: 481 us; the launch traced here: 472 us
  waiting for transfers between devices  307 us (64%)
  other arithmetic  113 us (23%)
  local copies, waits for them, and re-layouts  28.5 us (6%)
  between operations  16.8 us (3%)
  matrix products  5.65 us (1%)
    psum x4, waiting for transfers between devices, from_root(): return lax.psum(jnp.where(mine, shard, jnp.zeros_like(shard)), axis)  181 us
    all_gather x2, waiting for transfers between devices, on_device(): lax.all_gather(share.reshape(row_blocks, 1, block_size, half), 'row', axi...  85.2 us
    another operation x13, other arithmetic, factor_block(): lower_fac = jnp.linalg.cholesky(diag_block)  68.7 us
    another operation x5, other arithmetic, factor_block(): lax.linalg.triangular_solve(lower_fac, identity, left_side=True, lower=True)  39.4 us
    psum x1, waiting for transfers between devices, on_device(): head = lax.psum(update[:, :block_size], 'layer')  22.4 us
    reduce_scatter x1, waiting for transfers between devices, on_device(): lax.psum_scatter(total.reshape(rows, col_blocks, block_size), 'layer', sc...  17.9 us
  transfers between devices with their start and end apart: 8, of which 8 were waited for; matrix products, arithmetic and copies ran while one was open for 0% of the time, Pallas kernels for 0%

commit v1 on v0

--- a/solution.py
+++ b/solution.py
@@ -8,7 +8,7 @@
 
 def from_root(shard, axis, root):
     mine = lax.axis_index(axis) == root
-    return lax.psum(jnp.where(mine, shard, jnp.zeros_like(shard)), axis)
+    return jnp.sum(lax.all_gather(jnp.where(mine, shard, jnp.zeros_like(shard)), axis), axis=0)
 
 
 def factor_block(diag_block):

time: 481 us -> 386 us (0.80); the launches traced: 472 us -> 385 us
  waiting for transfers between devices: 307 us -> 219 us
  local copies, waits for them, and re-layouts: 28.5 us -> 15.5 us
  other arithmetic: 113 us -> 121 us
    psum x4 -> x0, waiting for transfers between devices: 181 us -> none  [from_root(): return lax.psum(jnp.where(mine, shard, jnp.zeros_like(shard)), axis)]
    all_gather x0 -> x2, waiting for transfers between devices: none -> 101 us  [from_root(): lax.all_gather(jnp.where(mine, shard, jnp.zeros_like(shard)), axis)]
    all_gather x2, waiting for transfers between devices: 85.2 us -> 77.8 us  [on_device(): lax.all_gather(share.reshape(row_blocks, 1, block_size, half), 'row', axi...]
    unnamed x16 -> x7, local copies, waits for them, and re-layouts: 6.78 us -> 1.32 us
    reduce_sum x0 -> x4, other arithmetic: none -> 4.85 us  [from_root(): jnp.sum(lax.all_gather(jnp.where(mine, shard, jnp.zeros_like(shard)), axi...]
  transfers between devices with their start and end apart: 8 -> 6, of which waited for: 8 -> 6; matrix products, arithmetic and copies ran while one was open for 0% -> 0% of each run, Pallas kernels for 0% -> 0%
where the time goes in v1:
time: 386 us; the launch traced here: 385 us
  waiting for transfers between devices  219 us (57%)
  other arithmetic  121 us (31%)
  between operations  16.5 us (4%)
  local copies, waits for them, and re-layouts  15.5 us (4%)
  matrix products  7.36 us (2%)
  blocking collectives  3.99 us (1%)
    all_gather x2, waiting for transfers between devices, from_root(): lax.all_gather(jnp.where(mine, shard, jnp.zeros_like(shard)), axis)  101 us
    all_gather x2, waiting for transfers between devices, on_device(): lax.all_gather(share.reshape(row_blocks, 1, block_size, half), 'row', axi...  77.8 us
    another operation x13, other arithmetic, factor_block(): lower_fac = jnp.linalg.cholesky(diag_block)  68.7 us
    another operation x5, other arithmetic, factor_block(): lax.linalg.triangular_solve(lower_fac, identity, left_side=True, lower=True)  40.2 us
    psum x1, waiting for transfers between devices, on_device(): head = lax.psum(update[:, :block_size], 'layer')  22.1 us
    reduce_scatter x1, waiting for transfers between devices, on_device(): lax.psum_scatter(total.reshape(rows, col_blocks, block_size), 'layer', sc...  18.4 us
    another operation x15, local copies, waits for them, and re-layouts, factor_block(): lax.linalg.triangular_solve(lower_fac, identity, left_side=True, lower=True)  8.21 us
  transfers between devices with their start and end apart: 6, of which 6 were waited for; matrix products, arithmetic and copies ran while one was open for 0% of the time, Pallas kernels for 0%

profile of v1, /device:TPU:0, one launch (start us, length us, event | category | flops | bytes accessed | tf_op | source)
XLA Modules:
  0.0 385.2 jit_solution(5795658071021773019)
XLA Ops:
  6.5 4.0 %reduce.8 = f32[256,4,256]{2,1,0:T(4,128)S(1)} reduce(f32[1,1,256,4,1,256]{5,4,3,2,1,0:T(1,128)} %param.4, f32[]{:T(128)} %constant.138), dimensions={0,1,4}, to_apply=%param.4.reduce_sub_computation | reduce | bytes 2097156 | tf_op args[0]
  11.8 51.7 %all-gather.11.cloned.1.call-done = f32[2048,256]{1,0:T(8,128)} async-done(((f32[256,256]{1,0:T(8,128)}), f32[2048,256]{1,0:T(8,128)}) %all-gather.11.cloned.1.call-update) | async-done | bytes 2097168 | tf_op jit(solution)/shard_map/all_gather | solution.py:11
  63.4 1.8 reduce_sum.36
  65.4 11.7 %cholesky.130 = f32[128,128]{1,0:T(8,128)S(1)} custom-call(f32[128,128]{1,0:T(8,128)S(1)} %cholesky.194), custom_call_target="Cholesky" | custom-call | tf_op jit(solution)/shard_map/jit(cholesky)/cholesky | solution.py:15
  77.1 9.8 %custom-call.13 = f32[1,128,128]{1,2,0:T(8,128)S(1)} custom-call(f32[1,128,128]{2,1,0:T(8,128)S(1)} %get-tuple-element.50), custom_call_target="InvertDiagBlocksLowerTriangular" | custom-call | tf_op jit(solution)/shard_map/jit(cholesky)/cholesky | solution.py:15
  87.5 11.7 %cholesky.147 = f32[128,128]{1,0:T(8,128)S(1)} custom-call(f32[128,128]{1,0:T(8,128)S(1)} %convolution_subtract_fusion.3), custom_call_target="Cholesky" | custom-call | tf_op jit(solution)/shard_map/jit(cholesky)/cholesky | solution.py:15
  101.4 4.3 %while.4 = (s32[]{:T(128)}, f32[256,256]{1,0:T(8,128)S(1)}, s32[2,2]{1,0:T(2,128)S(1)}, f32[2,128,128]{2,1,0:T(8,128)S(1)}, s32[]{:T(128)}) while((s32[]{:T(128)}, f32[256,256]{1,0:T(8,128)S(1)}, s32[2,2]{1,0:T(2,128)S(1)}, f32[2,128,128]{2,1,0:T(8,128)S(1)}, s32[]{:T(128)}) %tuple.46), condition=%wide.while_cond, body=%wide.while_body.sunk | while | flops 2 | bytes 131181 | solution.py:17
  102.3 1.4 bitcast_dynamic-update-slice_fusion.4
  104.3 1.4 bitcast_dynamic-update-slice_fusion.4
  105.7 19.7 %custom-call.14 = f32[2,128,128]{1,2,0:T(8,128)S(1)} custom-call(f32[2,128,128]{2,1,0:T(8,128)S(1)} %get-tuple-element.21), custom_call_target="InvertDiagBlocksLowerTriangular" | custom-call | tf_op jit(solution)/shard_map/triangular_solve/custom-call.0 | solution.py:17
  126.8 2.0 all-gather.1
  129.5 38.9 %all-gather.13.cloned.1.call-done = f32[2048,128]{1,0:T(8,128)} async-done(((f32[256,128]{1,0:T(8,128)}), f32[2048,128]{1,0:T(8,128)}) %all-gather.13.cloned.1.call-update) | async-done | bytes 1048592 | tf_op jit(solution)/shard_map/all_gather | solution.py:53
  168.4 1.1 constant_dynamic-slice_fusion.4
  169.5 1.9 fusion.36
  172.2 22.1 %all-reduce.3.cloned.1.call-done = f32[256,256]{1,0:T(8,128)} async-done(((f32[256,256]{1,0:T(8,128)}), f32[256,256]{1,0:T(8,128)}) %all-reduce.3.cloned.1.call-update) | async-done | bytes 262160 | tf_op jit(solution)/shard_map/psum | solution.py:68
  194.3 1.7 broadcast_select_fusion
  196.1 49.3 %all-gather.15.cloned.1.call-done = f32[2048,256]{1,0:T(8,128)} async-done(((f32[256,256]{1,0:T(8,128)}), f32[2048,256]{1,0:T(8,128)}) %all-gather.15.cloned.1.call-update) | async-done | bytes 2097168 | tf_op jit(solution)/shard_map/all_gather | solution.py:11
  245.4 1.8 reduce_sum.38
  247.4 11.7 %cholesky.164 = f32[128,128]{1,0:T(8,128)S(1)} custom-call(f32[128,128]{1,0:T(8,128)S(1)} %cholesky.197), custom_call_target="Cholesky" | custom-call | tf_op jit(solution)/shard_map/jit(cholesky)/cholesky | solution.py:15
  259.2 9.8 %custom-call.15 = f32[1,128,128]{1,2,0:T(8,128)S(1)} custom-call(f32[1,128,128]{2,1,0:T(8,128)S(1)} %get-tuple-element.46), custom_call_target="InvertDiagBlocksLowerTriangular" | custom-call | tf_op jit(solution)/shard_map/jit(cholesky)/cholesky | solution.py:15
  269.5 11.7 %cholesky.181 = f32[128,128]{1,0:T(8,128)S(1)} custom-call(f32[128,128]{1,0:T(8,128)S(1)} %convolution_subtract_fusion.2), custom_call_target="Cholesky" | custom-call | tf_op jit(solution)/shard_map/jit(cholesky)/cholesky | solution.py:15
  284.0 4.4 %while.5 = (s32[]{:T(128)}, f32[256,256]{1,0:T(8,128)S(1)}, s32[2,2]{1,0:T(2,128)S(1)}, f32[2,128,128]{2,1,0:T(8,128)S(1)}, s32[]{:T(128)}) while((s32[]{:T(128)}, f32[256,256]{1,0:T(8,128)S(1)}, s32[2,2]{1,0:T(2,128)S(1)}, f32[2,128,128]{2,1,0:T(8,128)S(1)}, s32[]{:T(128)}) %tuple.64), condition=%wide.while_cond.clone, body=%wide.while_body.clone.sunk | while | flops 2 | bytes 131181 | solution.py:17
  284.9 1.4 bitcast_dynamic-update-slice_fusion.5
  286.9 1.4 bitcast_dynamic-update-slice_fusion.5
  289.0 20.5 %custom-call.16 = f32[2,128,128]{1,2,0:T(8,128)S(1)} custom-call(f32[2,128,128]{2,1,0:T(8,128)} %copy-done.2), custom_call_target="InvertDiagBlocksLowerTriangular" | custom-call | tf_op jit(solution)/shard_map/triangular_solve/custom-call.0 | solution.py:17
  310.9 2.0 all-gather.4
  313.6 38.9 %all-gather.17.cloned.1.call-done = f32[2048,128]{1,0:T(8,128)} async-done(((f32[256,128]{1,0:T(8,128)}), f32[2048,128]{1,0:T(8,128)}) %all-gather.17.cloned.1.call-update) | async-done | bytes 1048592 | tf_op jit(solution)/shard_map/all_gather | solution.py:53
  353.6 1.9 convolution_add_fusion
  355.5 1.1 copy.16
  357.5 18.4 %reduce-scatter.2.cloned.1.call-done = f32[256,2,256]{2,0,1:T(8,128)} async-done(((f32[256,4,256]{2,0,1:T(8,128)}), f32[256,2,256]{2,0,1:T(8,128)}) %reduce-scatter.2.cloned.1.call-update) | async-done | bytes 524304 | tf_op jit(solution)/shard_map/reduce_scatter | solution.py:73
  375.9 1.2 fusion.2
  377.1 1.3 copy.10
  (72 shorter events, 14.8 us)
Async XLA Ops:
  6.5 56.9 %all-gather.11.cloned.1.call-start = ((), (), s32[]{:S(2)}) async-start(), calls=%async_computation.3 | async-start | bytes 2359296 | tf_op jit(solution)/shard_map/all_gather | solution.py:11
  11.5 157.0 %all-gather.13.cloned.1.call-start = ((), (), s32[]{:S(2)}) async-start(), calls=%async_computation.4 | async-start | bytes 1179648 | tf_op jit(solution)/shard_map/all_gather | solution.py:53
  129.5 64.8 %all-reduce.3.cloned.1.call-start = ((), (), s32[]{:S(2)}) async-start(), calls=%async_computation.1 | async-start | bytes 524288 | tf_op jit(solution)/shard_map/psum | solution.py:68
  172.2 73.3 %all-gather.15.cloned.1.call-start = ((), (), s32[]{:S(2)}) async-start(), calls=%async_computation.5 | async-start | bytes 2359296 | tf_op jit(solution)/shard_map/all_gather | solution.py:11
  196.0 156.5 %all-gather.17.cloned.1.call-start = ((), (), s32[]{:S(2)}) async-start(), calls=%async_computation.6 | async-start | bytes 1179648 | tf_op jit(solution)/shard_map/all_gather | solution.py:53
  247.4 63.0 %copy-start.1 = (f32[256,256]{1,0:T(8,128)S(1)}, f32[256,256]{1,0:T(8,128)}, u32[]{:S(2)}) copy-start(f32[256,256]{1,0:T(8,128)} %all-reduce.3.cloned.1.call-done) | copy-start | bytes 786436
  288.3 0.7 copy-start.2
  313.6 62.3 %reduce-scatter.2.cloned.1.call-start = ((), (), s32[]{:S(2)}) async-start(), calls=%async_computation.2 | async-start | bytes 1572864 | tf_op jit(solution)/shard_map/reduce_scatter | solution.py:73
  355.5 1.6 copy-start
Sparse Core Ops, SparseCore 0:
  11.6 51.8 all-gather.10
  129.6 38.7 all-gather.12
  172.3 21.9 all-reduce.2
  196.3 49.0 all-gather.14
  313.7 38.7 all-gather.16
  356.8 19.0 reduce-scatter.1
